TPU v7x, 256 devices: a whole 4x4x8 slice. The times are simulated.
256 devices in a mesh: grp: 32 (over x, z_hi, y), ep: 8 (over z_lo, core).
Axes of the slice: x: 4, y: 4, z: 8 (z_hi: 2, z_lo: 4; z = z_hi * 4 + z_lo), core: 2. Of those that a mesh axis runs over, the one named last changes fastest.
Arguments:
- queries: bfloat16 [1024, 2304], P('grp'), may hold values from -36 to 36, as said below
- residual: bfloat16 [1024, 2304], P(('grp', 'ep')), may hold values from -20 to 20
- gain: bfloat16 [2304], replicated, may hold values from 0.5 to 1.5
- key_pages: bfloat16 [2048, 128, 2304], P(('grp', 'ep')), may hold values from -6 to 6
- value_pages: bfloat16 [2048, 128, 2304], P(('grp', 'ep')), may hold values from -6 to 6
- page_table: int32 [1024, 32], P('grp'), may hold values from -1 to 63, as said below
- lengths: int32 [1024], P('grp'), may hold values from 1 to 4096, as said below
- split_flag: int32 [1024], P('grp'), may hold values from 0 to 1, as said below
- routes: int32 [1024, 2], P(('grp', 'ep')), may hold values from 0 to 7, all different within a row; in each aligned block of 4 rows (0 to 3, 4 to 7, ...) at most 2 rows name the same one
- gates: bfloat16 [1024, 2], P(('grp', 'ep')), may hold values from 0.19921875 to 1
- w_gate: bfloat16 [8, 2304, 5760], P('ep', None, 'grp'), may hold values from -0.125 to 0.125
- w_up: bfloat16 [8, 2304, 5760], P('ep', None, 'grp'), may hold values from -0.125 to 0.125
- w_down: bfloat16 [8, 5760, 2304], P('ep', 'grp'), may hold values from -0.078125 to 0.078125
Outputs:
- update: bfloat16 [1024, 2304], P(('grp', 'ep'))
Inputs may be any that keep to these rules, and one draw needn't show every extreme that they name: `page_table`: entries j with j * 128 < lengths[r] are pages of the row's group; no page is named twice within a group; the other entries are -1. `lengths`: A split request's first half, in the even group of its pair, is always 32 * 128 tokens; other rows are no longer. `split_flag`: in every group exactly one row is 1, at the same slot in both groups of each pair 2i, 2i + 1. `routes`: within the rows of one device no expert is named more than 2 times. `queries`: the two rows of a split request hold the same query.
All inputs are finite; a program needn't handle non-finite values.
Results may differ from a plain program's by a relative error of at most 0.015.
Values may be sent and summed in bfloat16 or wider, within the bound.
No kernel may reach another device: no remote copies, remote signals or barrier semaphores. Data moves between devices by JAX's collectives and lax.ppermute only.
A program may use at most 192 MiB of HBM per device.

v0:
```python
import jax
import jax.numpy as jnp
from jax import lax
from jax.sharding import PartitionSpec as P

HEAD_DIM = 64
PAGE = 128
NEG_FILL = -1e30
NORM_EPS = 1e-06


def joined_2(array, axis, combine):
    everything = jax.tree.map(lambda part: lax.all_gather(part, axis), array)
    leading = jax.tree.map(lambda part: part[0], everything)

    def turn(k, so_far):
        return combine(so_far, jax.tree.map(lambda part: part[k], everything))

    return lax.fori_loop(1, lax.axis_size(axis), turn, leading)


def from_partner(array, axis, bit):
    return lax.ppermute(array, axis, [(i, i ^ 1 << bit) for i in range(lax.axis_size(axis))])


def merge_parts(first_part, second_part):
    maxima_a, totals_a, weighted_a = first_part
    maxima_b, totals_b, weighted_b = second_part
    highest = jnp.maximum(maxima_a, maxima_b)
    factor_a = jnp.exp(maxima_a - highest)
    factor_b = jnp.exp(maxima_b - highest)
    head_count = maxima_a.shape[-1]
    shaped = weighted_a.shape
    wide = shaped[:-1] + (head_count, shaped[-1] // head_count)
    weighted = (
        weighted_a.reshape(wide) * factor_a[..., None]
        + weighted_b.reshape(wide) * factor_b[..., None]
    )
    return (highest, totals_a * factor_a + totals_b * factor_b, weighted.reshape(shaped))


def page_partials(group_q, page_rows, row_lengths, key_rows, value_rows, first_page):
    page_count = key_rows.shape[0]
    slot_count = group_q.shape[0]
    head_count = group_q.shape[1] // HEAD_DIM
    page_ids = first_page + jnp.arange(page_count, dtype=jnp.int32)
    table_steps = jnp.arange(page_rows.shape[1], dtype=jnp.int32)
    live_step = (table_steps * PAGE)[None, :] < row_lengths[:, None]
    matches = (page_rows[:, :, None] == page_ids[None, None, :]) & live_step[:, :, None]
    owned_page = jnp.any(matches, axis=1)
    where_at = jnp.sum(jnp.where(matches, table_steps[None, :, None], 0), axis=1)
    offsets = jnp.arange(PAGE, dtype=jnp.int32)
    token_pos = where_at[:, :, None] * PAGE + offsets[None, None, :]
    visible = (owned_page[:, :, None] & (token_pos < row_lengths[:, None, None])).reshape(
        slot_count, page_count * PAGE
    )
    query_heads = group_q.reshape(slot_count, head_count, HEAD_DIM)
    key_heads = key_rows.reshape(page_count * PAGE, head_count, HEAD_DIM)
    value_heads = value_rows.reshape(page_count * PAGE, head_count, HEAD_DIM)
    scores = jnp.einsum(
        "shd,khd->hsk", query_heads, key_heads, preferred_element_type=jnp.float32
    ) * HEAD_DIM ** (-0.5)
    scores = jnp.where(visible[None], scores, NEG_FILL)
    maxima = jnp.max(scores, axis=2)
    exp_terms = jnp.where(visible[None], jnp.exp(scores - maxima[..., None]), 0.0)
    totals = jnp.sum(exp_terms, axis=2)
    weights = exp_terms.astype(jnp.bfloat16)
    weighted = jnp.einsum("hsk,khd->shd", weights, value_heads, preferred_element_type=jnp.float32)
    return (maxima.T, totals.T, weighted.reshape(slot_count, head_count * HEAD_DIM))


def on_device(
    queries,
    residual,
    gain,
    key_pages,
    value_pages,
    page_table,
    lengths,
    split_flag,
    routes,
    gates,
    w_gate,
    w_up,
    w_down,
):
    req_dev = residual.shape[0]
    ep_size = lax.axis_size("ep")
    my_ep = lax.axis_index("ep")
    first_page = my_ep * key_pages.shape[0]
    maxima, totals, weighted = page_partials(
        queries, page_table, lengths, key_pages, value_pages, first_page
    )
    row_start = my_ep * req_dev
    merged = joined_2((maxima, totals, weighted), "ep", merge_parts)
    maxima = lax.dynamic_slice_in_dim(merged[0], row_start, req_dev, 0)
    totals = lax.dynamic_slice_in_dim(merged[1], row_start, req_dev, 0)
    weighted = lax.dynamic_slice_in_dim(merged[2], row_start, req_dev, 0)
    own_split = (lax.dynamic_slice_in_dim(split_flag, row_start, req_dev, 0) == 1)[:, None]
    partner = from_partner((maxima, totals, weighted), "grp", 0)
    joined = merge_parts((maxima, totals, weighted), partner)
    totals = jnp.where(own_split, joined[1], totals)
    weighted = jnp.where(own_split, joined[2], weighted)
    head_count = totals.shape[1]
    attn = (
        (weighted.reshape(req_dev, head_count, -1) / totals[..., None])
        .reshape(req_dev, -1)
        .astype(jnp.bfloat16)
    )
    stream = residual.astype(jnp.float32) + attn.astype(jnp.float32)
    normed = (
        stream
        * lax.rsqrt(jnp.mean(stream * stream, axis=-1, keepdims=True) + NORM_EPS)
        * gain.astype(jnp.float32)
    ).astype(jnp.bfloat16)
    capacity = max(2, (2 * req_dev + ep_size - 1) // ep_size)
    slot_count = ep_size * capacity
    chosen = routes.reshape(-1)
    one_hot = (chosen[:, None] == jnp.arange(ep_size, dtype=jnp.int32)[None, :]).astype(jnp.int32)
    ranking = jnp.sum((jnp.cumsum(one_hot, axis=0) - one_hot) * one_hot, axis=1)
    slot_of = chosen * capacity + ranking
    slot_ids = jnp.arange(slot_count, dtype=jnp.int32)
    placing = (slot_ids[:, None] == slot_of[None, :]).astype(jnp.bfloat16)
    doubled = jnp.repeat(normed, 2, axis=0)
    outgoing = (
        jnp.dot(placing, doubled, preferred_element_type=jnp.float32)
        .astype(jnp.bfloat16)
        .reshape(ep_size, capacity, -1)
    )
    arrived = lax.all_to_all(outgoing, "ep", split_axis=0, concat_axis=0, tiled=True).reshape(
        slot_count, -1
    )
    gate_matrix = w_gate[0]
    up_matrix = w_up[0]
    down_matrix = w_down[0]
    block_rows = lax.all_gather(arrived, "grp", axis=0, tiled=True)
    gate_part = jnp.dot(block_rows, gate_matrix, preferred_element_type=jnp.float32)
    up_part = jnp.dot(block_rows, up_matrix, preferred_element_type=jnp.float32)
    inner = (jax.nn.silu(gate_part) * up_part).astype(jnp.bfloat16)
    block_rows = inner
    summed = lax.psum_scatter(
        jnp.dot(block_rows, down_matrix, preferred_element_type=jnp.float32).astype(jnp.bfloat16),
        "grp",
        scatter_dimension=0,
        tiled=True,
    )
    results = summed.reshape(ep_size, capacity, -1)
    returned = lax.all_to_all(results, "ep", split_axis=0, concat_axis=0, tiled=True)
    picking = (slot_of[:, None] == slot_ids[None, :]).astype(jnp.float32) * gates.reshape(-1)[
        :, None
    ].astype(jnp.float32)
    blending = picking.reshape(req_dev, 2, slot_count).sum(axis=1).astype(jnp.bfloat16)
    mixture = jnp.dot(
        blending, returned.reshape(slot_count, -1), preferred_element_type=jnp.float32
    )
    return (attn.astype(jnp.float32) + mixture).astype(jnp.bfloat16)


def solution(mesh):
    in_specs = (
        P("grp", None),
        P(("grp", "ep"), None),
        P(),
        P(("grp", "ep"), None, None),
        P(("grp", "ep"), None, None),
        P("grp", None),
        P("grp"),
        P("grp"),
        P(("grp", "ep"), None),
        P(("grp", "ep"), None),
        P("ep", None, "grp"),
        P("ep", None, "grp"),
        P("ep", "grp", None),
    )
    out_specs = P(("grp", "ep"), None)
    return jax.shard_map(
        on_device, mesh=mesh, in_specs=in_specs, out_specs=out_specs, check_vma=False
    )
```

profile of v0, /device:TPU:1, one launch (start us, length us, event | category | flops | bytes accessed | tf_op | source)
XLA Modules:
  0.0 495.6 jit_solution(9139386518411092309)
XLA Ops:
  6.5 0.8 broadcast_compare_fusion
  7.4 1.4 select_reduce_fusion
  8.8 1.4 fusion.33
  10.2 7.1 %copy.64 = bf16[8,128,2304]{1,0,2:T(8,128)(2,1)} copy(bf16[8,128,2304]{2,1,0:T(8,128)(2,1)} %param.18) | data formatting | bytes 9437184 | tf_op args[3]
  17.3 8.2 %reshape.186 = bf16[1024,36,64]{0,2,1:T(8,128)(2,1)} reshape(bf16[8,128,2304]{1,0,2:T(8,128)(2,1)} %copy.64) | data formatting | bytes 9437184 | tf_op jit(solution)/shard_map/reshape | solution.py:58
  25.5 0.2 reshape.185
  25.8 7.0 %copy.68 = bf16[8,128,2304]{1,0,2:T(8,128)(2,1)} copy(bf16[8,128,2304]{2,1,0:T(8,128)(2,1)} %param.19) | data formatting | bytes 9437184 | tf_op args[4]
  32.8 8.2 %reshape.187 = bf16[1024,36,64]{0,2,1:T(8,128)(2,1)} reshape(bf16[8,128,2304]{1,0,2:T(8,128)(2,1)} %copy.68) | data formatting | bytes 9437184 | tf_op jit(solution)/shard_map/reshape | solution.py:59
  41.3 3.6 fusion.3
  45.0 1.4 fusion.14
  46.4 0.7 copy-done.1
  47.1 0.3 copy.69
  47.4 0.9 all_gather_reshape.3
  48.4 3.7 fusion.6
  52.2 17.1 %all-gather.1 = f32[256,36]{1,0:T(8,128)S(1)} all-gather(f32[32,36]{1,0:T(8,128)S(1)} %copy.67), channel_id=3, replica_groups=mesh['grp'=32,'ep'=8] {'ep'}, dimensions={0}, use_global_device_ids=true | all-gather | bytes 41472 | tf_op jit(solution)/shard_map/all_gather | solution.py:13
  69.4 14.3 %all-gather = f32[256,36]{1,0:T(8,128)S(1)} all-gather(f32[32,36]{1,0:T(8,128)S(1)} %copy.66), channel_id=2, replica_groups=mesh['grp'=32,'ep'=8] {'ep'}, dimensions={0}, use_global_device_ids=true | all-gather | bytes 41472 | tf_op jit(solution)/shard_map/all_gather | solution.py:13
  84.2 7.2 %all-gather.5.cloned.1.call-done = f32[8,32,2304]{2,1,0:T(8,128)} async-done(((f32[1,32,2304]{2,1,0:T(8,128)}), f32[8,32,2304]{2,1,0:T(8,128)}) %all-gather.5.cloned.1.call-update) | async-done | bytes 2359312 | tf_op jit(solution)/shard_map/all_gather | solution.py:13
  91.4 1.0 slice_bitcast_fusion
  92.4 13.8 %while.19 = (s32[]{:T(128)}, f32[32,36]{1,0:T(8,128)S(1)}, f32[32,36]{1,0:T(8,128)S(1)}, f32[32,2304]{1,0:T(8,128)S(1)}, f32[8,32,36]{2,1,0:T(8,128)S(1)}, /*ind...) while((s32[]{:T(128)}, f32[32,36]{1,0:T(8,128)S(1)}, ...), condition=%wide.region_5.6_spmd, body=%wide.region_4.5_spmd.sunk | while | flops 228101 | bytes 3290263 | solution.py:19
  92.5 0.2 mul.280
  92.7 0.2 mul.281
  92.9 0.2 mul.282
  93.1 0.2 mul.283
  93.3 1.1 fusion.58
  94.5 0.2 mul.280
  94.7 0.2 mul.281
  94.9 0.2 mul.282
  95.1 0.2 mul.283
  95.3 1.1 fusion.58
  96.4 0.2 mul.280
  96.7 0.2 mul.281
  96.9 0.2 mul.282
  97.1 0.2 mul.283
  97.3 1.1 fusion.58
  98.4 0.2 mul.280
  98.8 0.2 mul.282
  99.1 0.2 mul.283
  99.3 1.1 fusion.58
  100.4 0.2 mul.280
  100.8 0.2 mul.282
  101.2 1.1 fusion.58
  102.4 0.2 mul.280
  102.8 0.2 mul.282
  103.2 1.1 fusion.58
  104.4 0.2 mul.280
  104.8 0.2 mul.282
  105.2 1.1 fusion.58
  106.3 0.6 collective-permute-start
  106.9 1.0 collective-permute-start.2
  107.9 0.6 collective-permute-start.1
  108.5 0.4 collective-permute-done
  108.8 0.5 collective-permute-done.2
  110.0 0.8 collective-permute-done.1
  110.8 0.2 multiply_reduce_fusion
  111.3 11.3 %all_to_all.10 = bf16[8,2,2304]{2,1,0:T(2,128)(2,1)S(1)} all-to-all(bf16[8,2,2304]{2,1,0:T(2,128)(2,1)S(1)} %reshape.189), channel_id=1, replica_groups=mesh['grp'=32,'ep'=8] {'ep'}, dimensions={0} | all-to-all | bytes 147456 | tf_op jit(solution)/shard_map/all_to_all | solution.py:130
  122.7 0.7 reshape.190
  123.4 89.5 %all-gather.7.cloned.1.call-done = bf16[512,2304]{1,0:T(8,128)(2,1)} async-done(((bf16[16,2304]{1,0:T(8,128)(2,1)}), bf16[512,2304]{1,0:T(8,128)(2,1)}) %all-gather.7.cloned.1.call-update) | async-done | bytes 2359312 | tf_op jit(solution)/shard_map/all_gather | solution.py:136
  212.9 2.8 fusion.21
  215.7 4.9 convolution_convert_fusion
  220.7 254.7 %reduce-scatter.2.cloned.1.call-done = bf16[16,2304]{1,0:T(8,128)(2,1)} async-done(((bf16[512,2304]{1,0:T(8,128)(2,1)}), bf16[16,2304]{1,0:T(8,128)(2,1)}) %reduce-scatter.2.cloned.1.call-update) | async-done | bytes 73744 | tf_op jit(solution)/shard_map/reduce_scatter | solution.py:141
  475.4 1.5 reshape.191
  476.9 6.2 %all-to-all-start.1 = ((bf16[8,2,2304]{2,1,0:T(2,128)(2,1)}), bf16[8,2,2304]{2,1,0:T(2,128)(2,1)S(1)}, u32[]{:S(2)}, u32[]{:S(2)}) async-start(bf16[8,2,2304]{2,1,0:T(2,128)(2,1)} %reshape.191), calls=%async_computation.2 | async-start | bytes 147456 | tf_op jit(solution)/shard_map/all_to_all | solution.py:148
  483.3 5.0 %all-to-all-done.1 = bf16[8,2,2304]{2,1,0:T(2,128)(2,1)S(1)} async-done(((bf16[8,2,2304]{2,1,0:T(2,128)(2,1)}), bf16[8,2,2304]{2,1,0:T(2,128)(2,1)S(1)}, u32[]{:S(2)}, u32[]{:S(2)}) %all-to-all-start.1) | async-done | bytes 73760 | tf_op jit(solution)/shard_map/all_to_all | solution.py:148
  488.4 0.7 fusion.4
  (85 shorter events, 3.9 us)
Async XLA Ops:
  6.5 209.1 %copy-start = (bf16[1,180,2304]{2,1,0:T(8,128)(2,1)S(1)}, bf16[1,180,2304]{2,1,0:T(8,128)(2,1)}, u32[]{:S(2)}) copy-start(bf16[1,180,2304]{2,1,0:T(8,128)(2,1)} %param.27) | copy-start | bytes 2488324
  6.5 84.9 %all-gather.5.cloned.1.call-start = ((), (), s32[]{:S(2)}) async-start(), calls=%async_computation.3 | async-start | bytes 2654208 | tf_op jit(solution)/shard_map/all_gather | solution.py:13
  17.3 8.2 %copy-start.2 = (bf16[32,2304]{1,0:T(8,128)(2,1)S(1)}, bf16[32,2304]{1,0:T(8,128)(2,1)}, u32[]{:S(2)}) copy-start(bf16[32,2304]{1,0:T(8,128)(2,1)} %param.15) | copy-start | bytes 442372
  32.8 8.4 %copy-start.5 = (s32[32]{0:T(128)S(1)}, s32[32]{0:T(128)}, u32[]{:S(2)}) copy-start(s32[32]{0:T(128)} %param.21) | copy-start | bytes 388
  41.2 3.7 slice-start
  41.3 3.6 slice-start.1
  44.9 2.1 copy-start.1
  47.1 36.6 %copy-start.4 = (bf16[2304]{0:T(1024)(128)(2,1)S(1)}, bf16[2304]{0:T(1024)(128)(2,1)}, u32[]{:S(2)}) copy-start(bf16[2304]{0:T(1024)(128)(2,1)} %param.17) | copy-start | bytes 13828
  47.1 36.6 %copy-start.6 = (s32[4,2]{0,1:T(2,128)S(1)}, s32[4,2]{0,1:T(2,128)}, u32[]{:S(2)}) copy-start(s32[4,2]{0,1:T(2,128)} %param.23) | copy-start | bytes 100
  47.1 36.9 %copy-start.8 = (s32[32]{0:T(128)S(1)}, s32[32]{0:T(128)}, u32[]{:S(2)}) copy-start(s32[32]{0:T(128)} %param.22) | copy-start | bytes 388
  48.4 164.5 %all-gather.7.cloned.1.call-start = ((), (), s32[]{:S(2)}) async-start(), calls=%async_computation.4 | async-start | bytes 2433024 | tf_op jit(solution)/shard_map/all_gather | solution.py:136
  92.4 18.4 %copy-start.3 = (bf16[4,2304]{1,0:T(4,128)(2,1)S(1)}, bf16[4,2304]{1,0:T(4,128)(2,1)}, u32[]{:S(2)}) copy-start(bf16[4,2304]{1,0:T(4,128)(2,1)} %param.16) | copy-start | bytes 55300
  106.3 109.4 %copy-start.7 = (bf16[1,2304,180]{1,2,0:T(8,128)(2,1)S(1)}, bf16[1,2304,180]{1,2,0:T(8,128)(2,1)}, u32[]{:S(2)}) copy-start(bf16[1,2304,180]{1,2,0:T(8,128)(2,1)} %param.26) | copy-start | bytes 2488324
  106.3 2.5 collective-permute-start
  106.9 2.4 collective-permute-start.2
  107.9 2.9 collective-permute-start.1
  123.3 352.0 %reduce-scatter.2.cloned.1.call-start = ((), (), s32[]{:S(2)}) async-start(), calls=%async_computation.5 | async-start | bytes 2433024 | tf_op jit(solution)/shard_map/reduce_scatter | solution.py:141
  215.7 267.6 %copy-start.9 = (bf16[4,2]{0,1:T(2,128)(2,1)S(1)}, bf16[4,2]{0,1:T(2,128)(2,1)}, u32[]{:S(2)}) copy-start(bf16[4,2]{0,1:T(2,128)(2,1)} %param.24) | copy-start | bytes 52
  476.9 11.4 %all-to-all-start.1 = ((bf16[8,2,2304]{2,1,0:T(2,128)(2,1)}), bf16[8,2,2304]{2,1,0:T(2,128)(2,1)S(1)}, u32[]{:S(2)}, u32[]{:S(2)}) async-start(bf16[8,2,2304]{2,1,0:T(2,128)(2,1)} %reshape.191), calls=%async_computation.2 | async-start | bytes 147456 | tf_op jit(solution)/shard_map/all_to_all | solution.py:148
Sparse Core Ops, SparseCore 0:
  48.5 42.9 all-gather.4
  123.5 89.3 all-gather.6
  220.8 254.5 reduce-scatter.1
where the time goes:
time: 497 us; the launch traced here: 496 us
  waiting for transfers between devices  358 us (72%)
  local copies, waits for them, and re-layouts  43 us (9%)
  blocking collectives  42.7 us (9%)
  other arithmetic  16 us (3%)
  matrix products  13.6 us (3%)
  between operations  13.4 us (3%)
  starting transfers between devices  8.46 us (2%)
    reduce_scatter x1, waiting for transfers between devices, on_device(): lax.psum_scatter(jnp.dot(block_rows, down_matrix, preferred_element_type=...  255 us
    all_gather x1, waiting for transfers between devices, on_device(): block_rows = lax.all_gather(arrived, 'grp', axis=0, tiled=True)  89.5 us
    all_gather x2, blocking collectives, joined_2(): everything = jax.tree.map(lambda part: lax.all_gather(part, axis), array)  31.4 us
    unnamed x27, local copies, waits for them, and re-layouts  14.9 us
    all_to_all x1, blocking collectives, on_device(): lax.all_to_all(outgoing, 'ep', split_axis=0, concat_axis=0, tiled=True)  11.3 us
  transfers between devices with their start and end apart: 7, of which 7 were waited for; matrix products, arithmetic and copies ran while one was open for 1% of the time, Pallas kernels for 0%

commit v1 on v0

--- a/solution.py
+++ b/solution.py
@@ -133,7 +133,9 @@
     gate_matrix = w_gate[0]
     up_matrix = w_up[0]
     down_matrix = w_down[0]
-    block_rows = lax.all_gather(arrived, "grp", axis=0, tiled=True)
+    block_rows = jnp.concatenate(
+        lax.all_to_all(jnp.stack([arrived] * lax.axis_size("grp")), "grp", 0, 0), axis=0
+    )
     gate_part = jnp.dot(block_rows, gate_matrix, preferred_element_type=jnp.float32)
     up_part = jnp.dot(block_rows, up_matrix, preferred_element_type=jnp.float32)
     inner = (jax.nn.silu(gate_part) * up_part).astype(jnp.bfloat16)

time: 497 us -> 471 us (0.948)
  waiting for transfers between devices: 358 us -> 271 us
  blocking collectives: 42.7 us -> 106 us
    all_gather x1 -> x0, waiting for transfers between devices: 89.5 us -> none  [on_device(): block_rows = lax.all_gather(arrived, 'grp', axis=0, tiled=True)]
    all_to_all x0 -> x1, blocking collectives: none -> 62.9 us  [on_device(): lax.all_to_all(jnp.stack([arrived] * lax.axis_size('grp')), 'grp', 0, 0)]
  transfers between devices with their start and end apart: 7 -> 6, of which waited for: 7 -> 6; matrix products, arithmetic and copies ran while one was open for 1% -> 1% of each run, Pallas kernels for 0% -> 0%
where the time goes in v1:
time: 471 us; the launch traced here: 470 us
  waiting for transfers between devices  271 us (58%)
  blocking collectives  106 us (23%)
  local copies, waits for them, and re-layouts  42.5 us (9%)
  other arithmetic  16 us (3%)
  between operations  13.7 us (3%)
  matrix products  12.1 us (3%)
  starting transfers between devices  8.38 us (2%)
    reduce_scatter x1, waiting for transfers between devices, on_device(): lax.psum_scatter(jnp.dot(block_rows, down_matrix, preferred_element_type=...  257 us
    all_to_all x1, blocking collectives, on_device(): lax.all_to_all(jnp.stack([arrived] * lax.axis_size('grp')), 'grp', 0, 0)  62.9 us
    all_gather x2, blocking collectives, joined_2(): everything = jax.tree.map(lambda part: lax.all_gather(part, axis), array)  31.4 us
    unnamed x27, local copies, waits for them, and re-layouts  14.9 us
    all_to_all x1, blocking collectives, on_device(): lax.all_to_all(outgoing, 'ep', split_axis=0, concat_axis=0, tiled=True)  11.3 us
  transfers between devices with their start and end apart: 6, of which 6 were waited for; matrix products, arithmetic and copies ran while one was open for 1% of the time, Pallas kernels for 0%

profile of v1, /device:TPU:1, one launch (start us, length us, event | category | flops | bytes accessed | tf_op | source)
XLA Modules:
  0.0 470.1 jit_solution(114311291496405839)
XLA Ops:
  6.5 0.8 broadcast_compare_fusion
  7.4 1.4 select_reduce_fusion
  8.8 1.4 fusion.33
  10.2 7.1 %copy.64 = bf16[8,128,2304]{1,0,2:T(8,128)(2,1)} copy(bf16[8,128,2304]{2,1,0:T(8,128)(2,1)} %param.18) | data formatting | bytes 9437184 | tf_op args[3]
  17.3 8.2 %reshape.188 = bf16[1024,36,64]{0,2,1:T(8,128)(2,1)} reshape(bf16[8,128,2304]{1,0,2:T(8,128)(2,1)} %copy.64) | data formatting | bytes 9437184 | tf_op jit(solution)/shard_map/reshape | solution.py:58
  25.5 0.2 reshape.187
  25.7 7.0 %copy.68 = bf16[8,128,2304]{1,0,2:T(8,128)(2,1)} copy(bf16[8,128,2304]{2,1,0:T(8,128)(2,1)} %param.19) | data formatting | bytes 9437184 | tf_op args[4]
  32.7 8.2 %reshape.189 = bf16[1024,36,64]{0,2,1:T(8,128)(2,1)} reshape(bf16[8,128,2304]{1,0,2:T(8,128)(2,1)} %copy.68) | data formatting | bytes 9437184 | tf_op jit(solution)/shard_map/reshape | solution.py:59
  41.3 3.6 fusion.3
  45.0 1.4 fusion.14
  46.4 0.7 copy-done.1
  47.1 0.3 copy.69
  47.4 0.9 all_gather_reshape.3
  48.4 3.7 fusion.6
  52.1 17.1 %all-gather.1 = f32[256,36]{1,0:T(8,128)S(1)} all-gather(f32[32,36]{1,0:T(8,128)S(1)} %copy.67), channel_id=3, replica_groups=mesh['grp'=32,'ep'=8] {'ep'}, dimensions={0}, use_global_device_ids=true | all-gather | bytes 41472 | tf_op jit(solution)/shard_map/all_gather | solution.py:13
  69.3 14.3 %all-gather = f32[256,36]{1,0:T(8,128)S(1)} all-gather(f32[32,36]{1,0:T(8,128)S(1)} %copy.66), channel_id=2, replica_groups=mesh['grp'=32,'ep'=8] {'ep'}, dimensions={0}, use_global_device_ids=true | all-gather | bytes 41472 | tf_op jit(solution)/shard_map/all_gather | solution.py:13
  84.2 7.2 %all-gather.4.cloned.1.call-done = f32[8,32,2304]{2,1,0:T(8,128)} async-done(((f32[1,32,2304]{2,1,0:T(8,128)}), f32[8,32,2304]{2,1,0:T(8,128)}) %all-gather.4.cloned.1.call-update) | async-done | bytes 2359312 | tf_op jit(solution)/shard_map/all_gather | solution.py:13
  91.4 1.0 slice_bitcast_fusion
  92.4 13.8 %while.19 = (s32[]{:T(128)}, f32[32,36]{1,0:T(8,128)S(1)}, f32[32,36]{1,0:T(8,128)S(1)}, f32[32,2304]{1,0:T(8,128)S(1)}, f32[8,32,36]{2,1,0:T(8,128)S(1)}, /*ind...) while((s32[]{:T(128)}, f32[32,36]{1,0:T(8,128)S(1)}, ...), condition=%wide.region_5.6_spmd, body=%wide.region_4.5_spmd.sunk | while | flops 228101 | bytes 3290263 | solution.py:19
  92.5 0.2 mul.280
  92.7 0.2 mul.281
  92.9 0.2 mul.282
  93.1 0.2 mul.283
  93.3 1.1 fusion.58
  94.4 0.2 mul.280
  94.7 0.2 mul.281
  94.9 0.2 mul.282
  95.3 1.1 fusion.58
  96.4 0.2 mul.280
  96.8 0.2 mul.282
  97.1 0.2 mul.283
  97.3 1.1 fusion.58
  98.4 0.2 mul.280
  98.6 0.2 mul.281
  98.8 0.2 mul.282
  99.0 0.2 mul.283
  99.2 1.1 fusion.58
  100.4 0.2 mul.280
  100.6 0.2 mul.281
  100.8 0.2 mul.282
  101.0 0.2 mul.283
  101.2 1.1 fusion.58
  102.3 0.2 mul.280
  102.8 0.2 mul.282
  103.2 1.1 fusion.58
  104.3 0.2 mul.280
  104.7 0.2 mul.282
  105.2 1.1 fusion.58
  106.3 0.6 collective-permute-start
  106.9 1.0 collective-permute-start.2
  107.9 0.6 collective-permute-start.1
  108.4 0.4 collective-permute-done
  108.8 0.5 collective-permute-done.2
  109.9 0.8 collective-permute-done.1
  110.8 0.2 multiply_reduce_fusion
  111.3 11.3 %all_to_all.15 = bf16[8,2,2304]{2,1,0:T(2,128)(2,1)S(1)} all-to-all(bf16[8,2,2304]{2,1,0:T(2,128)(2,1)S(1)} %reshape.191), channel_id=1, replica_groups=mesh['grp'=32,'ep'=8] {'ep'}, dimensions={0} | all-to-all | bytes 147456 | tf_op jit(solution)/shard_map/all_to_all | solution.py:130
  122.8 62.9 %all_to_all.16 = bf16[32,16,2304]{2,1,0:T(8,128)(2,1)S(1)} all-to-all(bf16[32,16,2304]{2,1,0:T(8,128)(2,1)S(1)} %stack.3), channel_id=1, replica_groups=mesh['grp'=32,'ep'=8] {'grp'}, dimensions={0} | all-to-all | bytes 4718592 | tf_op jit(solution)/shard_map/all_to_all | solution.py:137
  185.8 1.7 fusion.21
  187.4 4.5 convolution_convert_fusion
  192.1 257.5 %reduce-scatter.2.cloned.1.call-done = bf16[16,2304]{1,0:T(8,128)(2,1)} async-done(((bf16[512,2304]{1,0:T(8,128)(2,1)}), bf16[16,2304]{1,0:T(8,128)(2,1)}) %reduce-scatter.2.cloned.1.call-update) | async-done | bytes 73744 | tf_op jit(solution)/shard_map/reduce_scatter | solution.py:143
  449.5 1.5 reshape.193
  451.1 6.2 %all-to-all-start.2 = ((bf16[8,2,2304]{2,1,0:T(2,128)(2,1)}), bf16[8,2,2304]{2,1,0:T(2,128)(2,1)S(1)}, u32[]{:S(2)}, u32[]{:S(2)}) async-start(bf16[8,2,2304]{2,1,0:T(2,128)(2,1)} %reshape.193), calls=%async_computation.3 | async-start | bytes 147456 | tf_op jit(solution)/shard_map/all_to_all | solution.py:150
  457.5 5.0 %all-to-all-done.2 = bf16[8,2,2304]{2,1,0:T(2,128)(2,1)S(1)} async-done(((bf16[8,2,2304]{2,1,0:T(2,128)(2,1)}), bf16[8,2,2304]{2,1,0:T(2,128)(2,1)S(1)}, u32[]{:S(2)}, u32[]{:S(2)}) %all-to-all-start.2) | async-done | bytes 73760 | tf_op jit(solution)/shard_map/all_to_all | solution.py:150
  462.5 0.7 fusion.4
  (84 shorter events, 3.8 us)
Async XLA Ops:
  6.5 180.9 %copy-start = (bf16[1,180,2304]{2,1,0:T(8,128)(2,1)S(1)}, bf16[1,180,2304]{2,1,0:T(8,128)(2,1)}, u32[]{:S(2)}) copy-start(bf16[1,180,2304]{2,1,0:T(8,128)(2,1)} %param.27) | copy-start | bytes 2488324
  6.5 84.9 %all-gather.4.cloned.1.call-start = ((), (), s32[]{:S(2)}) async-start(), calls=%async_computation.4 | async-start | bytes 2654208 | tf_op jit(solution)/shard_map/all_gather | solution.py:13
  17.3 8.2 %copy-start.2 = (bf16[32,2304]{1,0:T(8,128)(2,1)S(1)}, bf16[32,2304]{1,0:T(8,128)(2,1)}, u32[]{:S(2)}) copy-start(bf16[32,2304]{1,0:T(8,128)(2,1)} %param.15) | copy-start | bytes 442372
  32.7 8.4 %copy-start.5 = (s32[32]{0:T(128)S(1)}, s32[32]{0:T(128)}, u32[]{:S(2)}) copy-start(s32[32]{0:T(128)} %param.21) | copy-start | bytes 388
  41.2 3.7 slice-start
  41.3 3.6 slice-start.1
  44.9 2.1 copy-start.1
  47.1 36.6 %copy-start.4 = (bf16[2304]{0:T(1024)(128)(2,1)S(1)}, bf16[2304]{0:T(1024)(128)(2,1)}, u32[]{:S(2)}) copy-start(bf16[2304]{0:T(1024)(128)(2,1)} %param.17) | copy-start | bytes 13828
  47.1 36.6 %copy-start.6 = (s32[4,2]{0,1:T(2,128)S(1)}, s32[4,2]{0,1:T(2,128)}, u32[]{:S(2)}) copy-start(s32[4,2]{0,1:T(2,128)} %param.23) | copy-start | bytes 100
  47.1 36.8 %copy-start.8 = (s32[32]{0:T(128)S(1)}, s32[32]{0:T(128)}, u32[]{:S(2)}) copy-start(s32[32]{0:T(128)} %param.22) | copy-start | bytes 388
  48.3 401.2 %reduce-scatter.2.cloned.1.call-start = ((), (), s32[]{:S(2)}) async-start(), calls=%async_computation.5 | async-start | bytes 2433024 | tf_op jit(solution)/shard_map/reduce_scatter | solution.py:143
  92.4 18.4 %copy-start.3 = (bf16[4,2304]{1,0:T(4,128)(2,1)S(1)}, bf16[4,2304]{1,0:T(4,128)(2,1)}, u32[]{:S(2)}) copy-start(bf16[4,2304]{1,0:T(4,128)(2,1)} %param.16) | copy-start | bytes 55300
  106.3 2.5 collective-permute-start
  106.9 2.4 collective-permute-start.2
  107.9 2.9 collective-permute-start.1
  122.7 63.1 %copy-start.7 = (bf16[1,2304,180]{1,2,0:T(8,128)(2,1)S(1)}, bf16[1,2304,180]{1,2,0:T(8,128)(2,1)}, u32[]{:S(2)}) copy-start(bf16[1,2304,180]{1,2,0:T(8,128)(2,1)} %param.25) | copy-start | bytes 2488324
  187.4 270.0 %copy-start.9 = (bf16[4,2]{0,1:T(2,128)(2,1)S(1)}, bf16[4,2]{0,1:T(2,128)(2,1)}, u32[]{:S(2)}) copy-start(bf16[4,2]{0,1:T(2,128)(2,1)} %param.24) | copy-start | bytes 52
  451.1 11.4 %all-to-all-start.2 = ((bf16[8,2,2304]{2,1,0:T(2,128)(2,1)}), bf16[8,2,2304]{2,1,0:T(2,128)(2,1)S(1)}, u32[]{:S(2)}, u32[]{:S(2)}) async-start(bf16[8,2,2304]{2,1,0:T(2,128)(2,1)} %reshape.193), calls=%async_computation.3 | async-start | bytes 147456 | tf_op jit(solution)/shard_map/all_to_all | solution.py:150
Sparse Core Ops, SparseCore 0:
  48.5 42.9 all-gather.3
  192.1 257.4 reduce-scatter.1
